TPU v7x, 32 devices: a whole 2x2x4 slice. The times are simulated.
32 devices in a mesh: grp: 2 (over y), row: 4 (over x, core), col: 4 (over z).
Axes of the slice: x: 2, y: 2, z: 4, core: 2. Of those that a mesh axis runs over, the one named last changes fastest.
Arguments:
- programs: bfloat16 [2048, 2048], P(('grp', 'row'), 'col'), parts along dimension 0, may hold values from -6 to 6
- tests: bfloat16 [2048, 2048], P(('grp', 'col'), 'row'), parts along dimension 0, may hold values from -6 to 6
- weight: bfloat16 [2048, 2048], P('col', 'row'), may hold values from -0.125 to 0.125
- labels: int32 [2048, 1024], P(('grp', 'row'), 'col'), parts along dimension 0, may hold values 0 or 1
Outputs:
- grad_programs: bfloat16 [2048, 2048], P(('grp', 'row'), 'col'), parts along dimension 0
- grad_tests: bfloat16 [2048, 2048], P(('grp', 'col'), 'row'), parts along dimension 0
- grad_weight: float32 [4096, 2048], P(('grp', 'col'), 'row'), parts along dimension 0
There are 2 independent parts, one for each index of `grp`. A program takes and returns all parts, laid end to end along the dimension named above; an argument that names none is the same for every part. Nothing has to cross between parts.
All inputs are finite; a program needn't handle non-finite values. No bound on the sum of `labels` on one device may be relied on, other than what follows from the above.
Results may differ from a plain program's by a relative error of at most 0.017.
Values may be sent and summed in bfloat16 or wider, within the bound.
A program may use at most 64 MiB of HBM per device.

v0:
```python
import math
import jax
import jax.numpy as jnp
from jax import lax
from jax.sharding import PartitionSpec as P

E = 2048


def contract(left, right, left_dim, right_dim):
    return lax.dot_general(
        left, right, (((left_dim,), (right_dim,)), ((), ())), preferred_element_type=jnp.float32
    )


def local(programs, tests, weight, labels):
    factor = 1.0 / math.sqrt(E)
    targets = labels.astype(jnp.float32)
    w_rows = lax.all_gather(weight, "row", axis=1, tiled=True)
    share = lax.psum_scatter(
        jnp.dot(programs, w_rows, preferred_element_type=jnp.float32).astype(jnp.bfloat16),
        "col",
        scatter_dimension=0,
        tiled=True,
    )
    projected = lax.all_gather(share, "col", axis=0, tiled=True)
    test_whole = lax.all_gather(tests, "row", axis=1, tiled=True)
    logits = contract(projected, test_whole, 1, 1) * factor
    dlogits = (jax.nn.sigmoid(logits) - targets).astype(jnp.bfloat16)
    partial_sums = jnp.dot(dlogits, test_whole, preferred_element_type=jnp.float32)
    summed = lax.psum(partial_sums.astype(jnp.bfloat16), "col")
    grad_programs = (contract(summed, w_rows, 1, 1) * factor).astype(jnp.bfloat16)
    weight_part = contract(programs, summed, 0, 0) * factor
    test_part = contract(dlogits, projected, 0, 0) * factor
    grad_weight, test_total = (
        lax.psum_scatter(
            weight_part.astype(jnp.bfloat16), "row", scatter_dimension=1, tiled=True
        ).astype(jnp.float32),
        lax.psum_scatter(
            test_part.astype(jnp.bfloat16), "row", scatter_dimension=1, tiled=True
        ).astype(jnp.float32),
    )
    grad_tests = test_total.astype(jnp.bfloat16)
    return (grad_programs, grad_tests, grad_weight)


def solution(mesh):
    placed = (
        P(("grp", "row"), "col"),
        P(("grp", "col"), "row"),
        P("col", "row"),
        P(("grp", "row"), "col"),
    )
    return jax.shard_map(
        local,
        mesh=mesh,
        in_specs=placed,
        out_specs=(P(("grp", "row"), "col"), P(("grp", "col"), "row"), P(("grp", "col"), "row")),
        check_vma=False,
    )
```

profile of v0, /device:TPU:0, one launch (start us, length us, event | category | flops | bytes accessed | tf_op | source)
XLA Modules:
  0.0 236.3 jit_solution(9814701826729110321)
XLA Ops:
  7.2 0.0 copy-start
  7.2 0.0 all-gather.4.cloned.1.call-start
  7.2 0.7 all-gather.4.cloned.1.call-update
  7.9 0.0 copy-start.4
  7.9 0.0 reduce-scatter.4.cloned.1.call-start
  8.0 26.9 %all-gather.4.cloned.1.call-done = bf16[512,2048]{1,0:T(8,128)(2,1)} async-done(((bf16[512,512]{1,0:T(8,128)(2,1)}), bf16[512,2048]{1,0:T(8,128)(2,1)}) %all-gather.4.cloned.1.call-update) | async-done | bytes 2097168 | tf_op jit(solution)/shard_map/all_gather | solution.py:19
  34.9 0.0 copy-done
  34.9 3.3 %convolution_convert_fusion = bf16[256,2048]{1,0:T(8,128)(2,1)} fusion(bf16[256,512]{1,0:T(8,128)(2,1)S(1)} %copy-done, bf16[512,2048]{1,0:T(8,128)(2,1)} %all-gather.4.cloned.1.call-done), kind=kOutput, calls=%fused_computation.3 | convolution fusion | flops 537395200 | bytes 3407872 | tf_op jit(solution)/shard_map/dot_general | solution.py:21
  38.2 0.0 reduce-scatter.4.cloned.1.call-update
  38.2 0.0 all-gather.8.cloned.1.call-start
  38.2 0.7 all-gather.8.cloned.1.call-update
  38.9 0.0 all-gather.6.cloned.1.call-start
  39.0 26.5 %reduce-scatter.4.cloned.1.call-done = bf16[64,2048]{1,0:T(8,128)(2,1)} async-done(((bf16[256,2048]{1,0:T(8,128)(2,1)}), bf16[64,2048]{1,0:T(8,128)(2,1)}) %reduce-scatter.4.cloned.1.call-update) | async-done | bytes 262160 | tf_op jit(solution)/shard_map/reduce_scatter | solution.py:20
  65.5 0.0 all-gather.6.cloned.1.call-update
  65.5 0.0 all-reduce.2.cloned.1.call-start
  65.6 17.0 %all-gather.8.cloned.1.call-done = bf16[256,2048]{1,0:T(8,128)(2,1)} async-done(((bf16[256,512]{1,0:T(8,128)(2,1)}), bf16[256,2048]{1,0:T(8,128)(2,1)}) %all-gather.8.cloned.1.call-update) | async-done | bytes 1048592 | tf_op jit(solution)/shard_map/all_gather | solution.py:27
  82.5 0.0 copy-start.3
  82.6 29.5 %all-gather.6.cloned.1.call-done = bf16[256,2048]{1,0:T(8,128)(2,1)} async-done(((bf16[64,2048]{1,0:T(8,128)(2,1)}), bf16[256,2048]{1,0:T(8,128)(2,1)}) %all-gather.6.cloned.1.call-update) | async-done | bytes 1048592 | tf_op jit(solution)/shard_map/all_gather | solution.py:26
  112.0 0.0 copy-done.4
  112.0 2.0 fusion.8
  114.1 0.0 copy-done.3
  114.1 1.4 convolution_convert_fusion.1
  115.5 0.0 all-reduce.2.cloned.1.call-update
  115.5 0.0 reduce-scatter.8.cloned.1.call-start
  115.6 51.4 %all-reduce.2.cloned.1.call-done = bf16[256,2048]{1,0:T(8,128)(2,1)} async-done(((bf16[256,2048]{1,0:T(8,128)(2,1)}), bf16[256,2048]{1,0:T(8,128)(2,1)}) %all-reduce.2.cloned.1.call-update) | async-done | bytes 1048592 | tf_op jit(solution)/shard_map/psum | solution.py:31
  167.0 3.3 %fusion = bf16[512,2048]{0,1:T(8,128)(2,1)} fusion(bf16[256,2048]{1,0:T(8,128)(2,1)} %all-reduce.2.cloned.1.call-done, bf16[256,512]{1,0:T(8,128)(2,1)S(1)} %copy-done), kind=kOutput, calls=%fused_computation.1 | convolution fusion | flops 538968064 | bytes 3407872 | tf_op jit(solution)/shard_map/dot_general | solution.py:11
  170.3 0.0 copy-start.2
  170.3 0.0 reduce-scatter.8.cloned.1.call-update
  170.3 0.0 copy-start.1
  170.3 0.0 reduce-scatter.6.cloned.1.call-start
  170.4 1.1 copy-done.2
  171.5 1.4 fusion.1
  172.9 0.0 reduce-scatter.6.cloned.1.call-update
  173.0 0.0 copy-done.1
  173.0 2.7 %fusion.2 = bf16[256,512]{1,0:T(8,128)(2,1)} fusion(bf16[256,2048]{1,0:T(8,128)(2,1)} %all-reduce.2.cloned.1.call-done, bf16[512,2048]{1,0:T(8,128)(2,1)S(1)} %copy-done.1), kind=kOutput, calls=%fused_computation.7 | convolution fusion | flops 537133056 | bytes 3407872 | tf_op jit(solution)/shard_map/dot_general | solution.py:11
  175.6 25.6 %reduce-scatter.8.cloned.1.call-done = bf16[512,512]{0,1:T(8,128)(2,1)} async-done(((bf16[512,2048]{0,1:T(8,128)(2,1)}), bf16[512,512]{0,1:T(8,128)(2,1)}) %reduce-scatter.8.cloned.1.call-update) | async-done | bytes 524304 | tf_op jit(solution)/shard_map/reduce_scatter | solution.py:36
  201.3 2.2 copy.7
  203.5 25.9 %reduce-scatter.6.cloned.1.call-done = bf16[256,512]{1,0:T(8,128)(2,1)} async-done(((bf16[256,2048]{1,0:T(8,128)(2,1)}), bf16[256,512]{1,0:T(8,128)(2,1)}) %reduce-scatter.6.cloned.1.call-update) | async-done | bytes 262160 | tf_op jit(solution)/shard_map/reduce_scatter | solution.py:39
Async XLA Ops:
  7.2 27.7 %copy-start = (bf16[256,512]{1,0:T(8,128)(2,1)S(1)}, bf16[256,512]{1,0:T(8,128)(2,1)}, u32[]{:S(2)}) copy-start(bf16[256,512]{1,0:T(8,128)(2,1)} %param.4) | copy-start | bytes 786436
  7.2 27.7 %all-gather.4.cloned.1.call-start = ((), (), s32[]{:S(2)}) async-start(), calls=%async_computation.3 | async-start | bytes 2621440 | tf_op jit(solution)/shard_map/all_gather | solution.py:19
  7.9 104.1 %copy-start.4 = (s32[256,256]{1,0:T(8,128)S(1)}, s32[256,256]{1,0:T(8,128)}, u32[]{:S(2)}) copy-start(s32[256,256]{1,0:T(8,128)} %param.7) | copy-start | bytes 786436
  7.9 57.6 %reduce-scatter.4.cloned.1.call-start = ((), (), s32[]{:S(2)}) async-start(), calls=%async_computation.4 | async-start | bytes 1310720 | tf_op jit(solution)/shard_map/reduce_scatter | solution.py:20
  38.2 44.4 %all-gather.8.cloned.1.call-start = ((), (), s32[]{:S(2)}) async-start(), calls=%async_computation.6 | async-start | bytes 1310720 | tf_op jit(solution)/shard_map/all_gather | solution.py:27
  38.9 73.1 %all-gather.6.cloned.1.call-start = ((), (), s32[]{:S(2)}) async-start(), calls=%async_computation.5 | async-start | bytes 1310720 | tf_op jit(solution)/shard_map/all_gather | solution.py:26
  65.5 101.5 %all-reduce.2.cloned.1.call-start = ((), (), s32[]{:S(2)}) async-start(), calls=%async_computation.7 | async-start | bytes 2097152 | tf_op jit(solution)/shard_map/psum | solution.py:31
  82.5 31.5 %copy-start.3 = (bf16[256,2048]{1,0:T(8,128)(2,1)S(1)}, bf16[256,2048]{1,0:T(8,128)(2,1)}, u32[]{:S(2)}) copy-start(bf16[256,2048]{1,0:T(8,128)(2,1)} %all-gather.8.cloned.1.call-done) | copy-start | bytes 3145732
  115.5 85.7 %reduce-scatter.8.cloned.1.call-start = ((), (), s32[]{:S(2)}) async-start(), calls=%async_computation.9 | async-start | bytes 2621440 | tf_op jit(solution)/shard_map/reduce_scatter | solution.py:36
  170.3 1.2 copy-start.2
  170.3 2.7 %copy-start.1 = (bf16[512,2048]{1,0:T(8,128)(2,1)S(1)}, bf16[512,2048]{1,0:T(8,128)(2,1)}, u32[]{:S(2)}) copy-start(bf16[512,2048]{1,0:T(8,128)(2,1)} %all-gather.4.cloned.1.call-done) | copy-start | bytes 6291460
  170.3 59.1 %reduce-scatter.6.cloned.1.call-start = ((), (), s32[]{:S(2)}) async-start(), calls=%async_computation.8 | async-start | bytes 1310720 | tf_op jit(solution)/shard_map/reduce_scatter | solution.py:39
Sparse Core Ops, SparseCore 0:
  9.6 25.2 all-gather.3
  38.3 27.1 reduce-scatter.3
  67.1 15.3 all-gather.7
  84.1 27.9 all-gather.5
  115.6 51.3 all-reduce.1
  170.4 30.7 reduce-scatter.7
  204.5 24.8 reduce-scatter.5
where the time goes:
time: 237 us; the launch traced here: 236 us
  waiting for transfers between devices  204 us (86%)
  between operations  14.2 us (6%)
  matrix products  14.1 us (6%)
  local copies, waits for them, and re-layouts  3.38 us (1%)
    psum x1, waiting for transfers between devices, local(): summed = lax.psum(partial_sums.astype(jnp.bfloat16), 'col')  51.4 us
    all_gather x1, waiting for transfers between devices, local(): projected = lax.all_gather(share, 'col', axis=0, tiled=True)  29.5 us
    all_gather x1, waiting for transfers between devices, local(): w_rows = lax.all_gather(weight, 'row', axis=1, tiled=True)  26.9 us
    reduce_scatter x1, waiting for transfers between devices, local(): lax.psum_scatter(jnp.dot(programs, w_rows, preferred_element_type=jnp.flo...  26.5 us
    reduce_scatter x1, waiting for transfers between devices, local(): lax.psum_scatter(test_part.astype(jnp.bfloat16), 'row', scatter_dimension...  25.9 us
    reduce_scatter x1, waiting for transfers between devices, local(): lax.psum_scatter(weight_part.astype(jnp.bfloat16), 'row', scatter_dimensi...  25.6 us
    all_gather x1, waiting for transfers between devices, local(): test_whole = lax.all_gather(tests, 'row', axis=1, tiled=True)  17 us
    dot_general x4, matrix products, contract(): lax.dot_general(left, right, (((left_dim,), (right_dim,)), ((), ())), pre...  9.44 us
  transfers between devices with their start and end apart: 7, of which 7 were waited for; matrix products, arithmetic and copies ran while one was open for 3% of the time, Pallas kernels for 0%

commit v1 on v0

--- a/solution.py
+++ b/solution.py
@@ -23,7 +23,12 @@
         scatter_dimension=0,
         tiled=True,
     )
-    projected = lax.all_gather(share, "col", axis=0, tiled=True)
+    ring = [share]
+    for hop in range(3):
+        ring.append(lax.ppermute(ring[-1], "col", [(dev, (dev + 1) % 4) for dev in range(4)]))
+    projected = jnp.roll(
+        jnp.concatenate(ring[::-1], axis=0), (lax.axis_index("col") + 1) * ring[0].shape[0], axis=0
+    )
     test_whole = lax.all_gather(tests, "row", axis=1, tiled=True)
     logits = contract(projected, test_whole, 1, 1) * factor
     dlogits = (jax.nn.sigmoid(logits) - targets).astype(jnp.bfloat16)

time: 237 us -> 227 us (0.958)
  waiting for transfers between devices: 204 us -> 195 us
    all_gather x1 -> x0, waiting for transfers between devices: 29.5 us -> none  [local(): projected = lax.all_gather(share, 'col', axis=0, tiled=True)]
    ppermute x0 -> x3, waiting for transfers between devices: none -> 26.8 us  [local(): lax.ppermute(ring[-1], 'col', [(dev, (dev + 1) % 4) for dev in range(4)])]
    all_gather x1, waiting for transfers between devices: 17 us -> 8.91 us  [local(): test_whole = lax.all_gather(tests, 'row', axis=1, tiled=True)]
  transfers between devices with their start and end apart: 7 -> 9, of which waited for: 7 -> 9; matrix products, arithmetic and copies ran while one was open for 3% -> 3% of each run, Pallas kernels for 0% -> 0%
where the time goes in v1:
time: 227 us
  waiting for transfers between devices  195 us (86%)
  between operations  14.3 us (6%)
  matrix products  14.2 us (6%)
  local copies, waits for them, and re-layouts  3.36 us (1%)
    psum x1, waiting for transfers between devices, local(): summed = lax.psum(partial_sums.astype(jnp.bfloat16), 'col')  51.9 us
    reduce_scatter x1, waiting for transfers between devices, local(): lax.psum_scatter(jnp.dot(programs, w_rows, preferred_element_type=jnp.flo...  27.2 us
    all_gather x1, waiting for transfers between devices, local(): w_rows = lax.all_gather(weight, 'row', axis=1, tiled=True)  26.9 us
    ppermute x3, waiting for transfers between devices, local(): lax.ppermute(ring[-1], 'col', [(dev, (dev + 1) % 4) for dev in range(4)])  26.8 us
    reduce_scatter x1, waiting for transfers between devices, local(): lax.psum_scatter(weight_part.astype(jnp.bfloat16), 'row', scatter_dimensi...  26.5 us
    reduce_scatter x1, waiting for transfers between devices, local(): lax.psum_scatter(test_part.astype(jnp.bfloat16), 'row', scatter_dimension...  25.8 us
    dot_general x4, matrix products, contract(): lax.dot_general(left, right, (((left_dim,), (right_dim,)), ((), ())), pre...  9.46 us
    all_gather x1, waiting for transfers between devices, local(): test_whole = lax.all_gather(tests, 'row', axis=1, tiled=True)  8.91 us
  transfers between devices with their start and end apart: 9, of which 9 were waited for; matrix products, arithmetic and copies ran while one was open for 3% of the time, Pallas kernels for 0%

profile of v1, /device:TPU:0, one launch (start us, length us, event | category | flops | bytes accessed | tf_op | source)
XLA Modules:
  0.0 226.9 jit_solution(1429538750219710598)
XLA Ops:
  7.2 0.0 copy-start
  7.2 0.0 all-gather.3.cloned.1.call-start
  7.2 0.7 all-gather.3.cloned.1.call-update
  7.9 0.0 reduce-scatter.4.cloned.1.call-start
  8.0 26.9 %all-gather.3.cloned.1.call-done = bf16[512,2048]{1,0:T(8,128)(2,1)} async-done(((bf16[512,512]{1,0:T(8,128)(2,1)}), bf16[512,2048]{1,0:T(8,128)(2,1)}) %all-gather.3.cloned.1.call-update) | async-done | bytes 2097168 | tf_op jit(solution)/shard_map/all_gather | solution.py:19
  34.9 0.0 copy-done
  34.9 3.3 %convolution_convert_fusion = bf16[256,2048]{1,0:T(8,128)(2,1)} fusion(bf16[256,512]{1,0:T(8,128)(2,1)S(1)} %copy-done, bf16[512,2048]{1,0:T(8,128)(2,1)} %all-gather.3.cloned.1.call-done), kind=kOutput, calls=%fused_computation.3 | convolution fusion | flops 537395200 | bytes 3407872 | tf_op jit(solution)/shard_map/dot_general | solution.py:21
  38.2 0.0 reduce-scatter.4.cloned.1.call-update
  38.2 0.0 all-gather.5.cloned.1.call-start
  38.2 27.2 %reduce-scatter.4.cloned.1.call-done = bf16[64,2048]{1,0:T(8,128)(2,1)} async-done(((bf16[256,2048]{1,0:T(8,128)(2,1)}), bf16[64,2048]{1,0:T(8,128)(2,1)}) %reduce-scatter.4.cloned.1.call-update) | async-done | bytes 262160 | tf_op jit(solution)/shard_map/reduce_scatter | solution.py:20
  65.5 0.0 copy-start.3
  65.5 0.0 collective-permute-start
  65.5 9.9 %collective-permute-done = bf16[64,2048]{1,0:T(8,128)(2,1)S(1)} collective-permute-done((bf16[64,2048]{1,0:T(8,128)(2,1)}, bf16[64,2048]{1,0:T(8,128)(2,1)S(1)}, u32[]{:S(2)}, u32[]{:S(2)}) %collective-permute-start) | collective-permute-done | bytes 262176 | tf_op jit(solution)/shard_map/ppermute | solution.py:28
  75.4 0.0 collective-permute-start.1
  75.4 8.8 %collective-permute-done.1 = bf16[64,2048]{1,0:T(8,128)(2,1)S(1)} collective-permute-done((bf16[64,2048]{1,0:T(8,128)(2,1)S(1)}, bf16[64,2048]{1,0:T(8,128)(2,1)S(1)}, u32[]{:S(2)}, u32[]{:S(2)}) %collective-permute-start.1) | collective-permute-done | bytes 262176 | tf_op jit(solution)/shard_map/ppermute | solution.py:28
  84.2 0.0 collective-permute-start.2
  84.2 0.0 all-gather.5.cloned.1.call-update
  84.2 0.0 all-reduce.2.cloned.1.call-start
  84.3 8.1 %collective-permute-done.2 = bf16[64,2048]{1,0:T(8,128)(2,1)S(1)} collective-permute-done((bf16[64,2048]{1,0:T(8,128)(2,1)S(1)}, bf16[64,2048]{1,0:T(8,128)(2,1)S(1)}, u32[]{:S(2)}, u32[]{:S(2)}) %collective-permute-start.2) | collective-permute-done | bytes 262176 | tf_op jit(solution)/shard_map/ppermute | solution.py:28
  92.4 1.0 constant_dynamic-update-slice_fusion.4
  93.5 0.0 copy-done.3
  93.5 0.0 copy-start.4
  93.5 8.9 %all-gather.5.cloned.1.call-done = bf16[256,2048]{1,0:T(8,128)(2,1)} async-done(((bf16[256,512]{1,0:T(8,128)(2,1)}), bf16[256,2048]{1,0:T(8,128)(2,1)}) %all-gather.5.cloned.1.call-update) | async-done | bytes 1048592 | tf_op jit(solution)/shard_map/all_gather | solution.py:32
  102.4 0.0 copy-start.2
  102.4 1.8 fusion.8
  104.3 0.0 copy-done.2
  104.3 1.4 convolution_convert_fusion.1
  105.7 0.0 copy-done.4
  105.7 0.0 all-reduce.2.cloned.1.call-update
  105.7 0.0 reduce-scatter.8.cloned.1.call-start
  105.8 51.9 %all-reduce.2.cloned.1.call-done = bf16[256,2048]{1,0:T(8,128)(2,1)} async-done(((bf16[256,2048]{1,0:T(8,128)(2,1)}), bf16[256,2048]{1,0:T(8,128)(2,1)}) %all-reduce.2.cloned.1.call-update) | async-done | bytes 1048592 | tf_op jit(solution)/shard_map/psum | solution.py:36
  157.7 3.3 %fusion = bf16[512,2048]{0,1:T(8,128)(2,1)} fusion(bf16[256,2048]{1,0:T(8,128)(2,1)} %all-reduce.2.cloned.1.call-done, bf16[256,512]{1,0:T(8,128)(2,1)S(1)} %copy-done), kind=kOutput, calls=%fused_computation.1 | convolution fusion | flops 538968064 | bytes 3407872 | tf_op jit(solution)/shard_map/dot_general | solution.py:11
  161.0 0.0 reduce-scatter.8.cloned.1.call-update
  161.1 0.0 copy-start.1
  161.1 0.0 copy-start.5
  161.1 0.0 reduce-scatter.6.cloned.1.call-start
  161.1 2.9 %fusion.1 = bf16[256,2048]{1,0:T(8,128)(2,1)} fusion(bf16[256,256]{1,0:T(8,128)(2,1)S(1)} %fusion.8, bf16[512,2048]{1,0:T(8,128)(2,1)} %copy-done.4, s32[]{:T(128)S(6)} %select_n.14), kind=kOutput, calls=%fused_computation.4 | convolution fusion | flops 269484032 | bytes 2228228 | tf_op jit(solution)/shard_map/dot_general | solution.py:11
  164.0 0.0 reduce-scatter.6.cloned.1.call-update
  164.0 0.0 copy-done.1
  164.0 0.0 copy-done.5
  164.0 1.5 fusion.2
  165.5 26.5 %reduce-scatter.8.cloned.1.call-done = bf16[512,512]{0,1:T(8,128)(2,1)} async-done(((bf16[512,2048]{0,1:T(8,128)(2,1)}), bf16[512,512]{0,1:T(8,128)(2,1)}) %reduce-scatter.8.cloned.1.call-update) | async-done | bytes 524304 | tf_op jit(solution)/shard_map/reduce_scatter | solution.py:41
  192.0 2.2 copy.7
  194.2 25.8 %reduce-scatter.6.cloned.1.call-done = bf16[256,512]{1,0:T(8,128)(2,1)} async-done(((bf16[256,2048]{1,0:T(8,128)(2,1)}), bf16[256,512]{1,0:T(8,128)(2,1)}) %reduce-scatter.6.cloned.1.call-update) | async-done | bytes 262160 | tf_op jit(solution)/shard_map/reduce_scatter | solution.py:44
  (7 shorter events, 0.1 us)
Async XLA Ops:
  7.2 27.7 %copy-start = (bf16[256,512]{1,0:T(8,128)(2,1)S(1)}, bf16[256,512]{1,0:T(8,128)(2,1)}, u32[]{:S(2)}) copy-start(bf16[256,512]{1,0:T(8,128)(2,1)} %param.4) | copy-start | bytes 786436
  7.2 27.7 %all-gather.3.cloned.1.call-start = ((), (), s32[]{:S(2)}) async-start(), calls=%async_computation.3 | async-start | bytes 2621440 | tf_op jit(solution)/shard_map/all_gather | solution.py:19
  7.9 57.6 %reduce-scatter.4.cloned.1.call-start = ((), (), s32[]{:S(2)}) async-start(), calls=%async_computation.4 | async-start | bytes 1310720 | tf_op jit(solution)/shard_map/reduce_scatter | solution.py:20
  38.2 64.2 %all-gather.5.cloned.1.call-start = ((), (), s32[]{:S(2)}) async-start(), calls=%async_computation.5 | async-start | bytes 1310720 | tf_op jit(solution)/shard_map/all_gather | solution.py:32
  65.5 28.0 %copy-start.3 = (bf16[64,2048]{1,0:T(8,128)(2,1)S(1)}, bf16[64,2048]{1,0:T(8,128)(2,1)}, u32[]{:S(2)}) copy-start(bf16[64,2048]{1,0:T(8,128)(2,1)} %reduce-scatter.4.cloned.1.call-done) | copy-start | bytes 786436
  65.5 9.9 %collective-permute-start = (bf16[64,2048]{1,0:T(8,128)(2,1)}, bf16[64,2048]{1,0:T(8,128)(2,1)S(1)}, u32[]{:S(2)}, u32[]{:S(2)}) collective-permute-start(bf16[64,2048]{1,0:T(8,128)(2,1)} %reduce-scatter.4.cloned.1.call-done), channel_id=1, source_target_pairs={{0,1},{1,2},{2,3},{3,0},{4,5},{5,6},{6,7},{7,4},{8,9},{9,10},{10,1... | collective-permute-start | bytes 786440 | tf_op jit(solution)/shard_map/ppermute | solution.py:28
  75.4 8.8 %collective-permute-start.1 = (bf16[64,2048]{1,0:T(8,128)(2,1)S(1)}, bf16[64,2048]{1,0:T(8,128)(2,1)S(1)}, u32[]{:S(2)}, u32[]{:S(2)}) collective-permute-start(bf16[64,2048]{1,0:T(8,128)(2,1)S(1)} %collective-permute-done), channel_id=1, source_target_pairs={{0,1},{1,2},{2,3},{3,0},{4,5},{5,6},{6,7},{7,4},{8,9},{9,10},{10,1... | collective-permute-start | bytes 786440 | tf_op jit(solution)/shard_map/ppermute | solution.py:28
  84.2 8.2 %collective-permute-start.2 = (bf16[64,2048]{1,0:T(8,128)(2,1)S(1)}, bf16[64,2048]{1,0:T(8,128)(2,1)S(1)}, u32[]{:S(2)}, u32[]{:S(2)}) collective-permute-start(bf16[64,2048]{1,0:T(8,128)(2,1)S(1)} %collective-permute-done.1), channel_id=1, source_target_pairs={{0,1},{1,2},{2,3},{3,0},{4,5},{5,6},{6,7},{7,4},{8,9},{9,10},{10,1... | collective-permute-start | bytes 786440 | tf_op jit(solution)/shard_map/ppermute | solution.py:28
  84.2 73.5 %all-reduce.2.cloned.1.call-start = ((), (), s32[]{:S(2)}) async-start(), calls=%async_computation.6 | async-start | bytes 2097152 | tf_op jit(solution)/shard_map/psum | solution.py:36
  93.5 12.2 %copy-start.4 = (bf16[512,2048]{1,0:T(8,128)(2,1)}, bf16[512,2048]{1,0:T(8,128)(2,1)S(1)}, u32[]{:S(2)}) copy-start(bf16[512,2048]{1,0:T(8,128)(2,1)S(1)} %constant_dynamic-update-slice_fusion) | copy-start | bytes 6291460
  102.4 1.9 copy-start.2
  105.7 86.3 %reduce-scatter.8.cloned.1.call-start = ((), (), s32[]{:S(2)}) async-start(), calls=%async_computation.8 | async-start | bytes 2621440 | tf_op jit(solution)/shard_map/reduce_scatter | solution.py:41
  161.1 3.0 %copy-start.1 = (bf16[512,2048]{1,0:T(8,128)(2,1)S(1)}, bf16[512,2048]{1,0:T(8,128)(2,1)}, u32[]{:S(2)}) copy-start(bf16[512,2048]{1,0:T(8,128)(2,1)} %all-gather.3.cloned.1.call-done) | copy-start | bytes 6291460
  161.1 3.0 %copy-start.5 = (bf16[256,2048]{1,0:T(8,128)(2,1)S(1)}, bf16[256,2048]{1,0:T(8,128)(2,1)}, u32[]{:S(2)}) copy-start(bf16[256,2048]{1,0:T(8,128)(2,1)} %all-reduce.2.cloned.1.call-done) | copy-start | bytes 3145732
  161.1 59.0 %reduce-scatter.6.cloned.1.call-start = ((), (), s32[]{:S(2)}) async-start(), calls=%async_computation.7 | async-start | bytes 1310720 | tf_op jit(solution)/shard_map/reduce_scatter | solution.py:44
Sparse Core Ops, SparseCore 0:
  9.6 25.2 all-gather.2
  38.3 27.1 reduce-scatter.3
  84.3 18.0 all-gather.4
  105.9 51.8 all-reduce.1
  161.2 30.7 reduce-scatter.7
  195.1 24.8 reduce-scatter.5
